TPU v7x, 128 devices: a whole 4x4x4 slice. The times are simulated.
128 devices in a mesh: sky: 16 (over z, x), src: 8 (over y, core).
Axes of the slice: x: 4, y: 4, z: 4, core: 2. Of those that a mesh axis runs over, the one named last changes fastest.
Arguments:
- exposures: float32 [16, 128, 256, 256], P('sky', 'src'), may hold values from -6 to 6
- variance: float32 [16, 128, 256, 256], P('sky', 'src'), may hold values from 0.25 to 4
- coef_table: float32 [64, 45], replicated, may hold values from -6 to 6
- coef_index: int32 [16, 128], P('sky', 'src'), may hold values from 0 to 63
- offsets: int32 [16, 128, 2], P('sky', 'src'), may hold values from 0 to 256
- tile_codes: int32 [16, 128], P('sky', 'src'), may hold values from 0 to 15, as said below
- detect_ra: float32 [41], replicated, may hold values from -1 to 1
- detect_dec: float32 [41], replicated, may hold values from -1 to 1
Outputs:
- coadd: float32 [8192, 4096], P('sky', 'src')
- detection: float32 [8192, 4096], P('sky', 'src')
Inputs may be any that keep to these rules, and one draw needn't show every extreme that they name: `tile_codes`: code c sends a tile to the patch row c // 8 after the holder's own (wrapping around) and to owner c mod 8 along src. On one device at most 2 tiles name the same code; in every sky row one code is named by exactly 2 tiles on every device of that row.
All inputs are finite; a program needn't handle non-finite values.
Results may differ from a plain program's by a relative error of at most 0.0003.
Values sent between devices are 32-bit elements; how exact they have to be, the bound alone decides.
No kernel may reach another device: no remote copies, remote signals or barrier semaphores. Data moves between devices by JAX's collectives and lax.ppermute only.
A program may use at most 192 MiB of HBM per device.

v0:
```python
import jax
import jax.numpy as jnp
from jax import lax
from jax.sharding import PartitionSpec as P

TILE = 256
PATCH = 512
CAP = 2
KSIZE = 21
DSIZE = 41
RIM = 20


SPREADS = (0.75, 1.5, 3.0)


def from_behind(value, axis, steps):
    count = lax.axis_size(axis)
    pairs = [(source, (source + steps) % count) for source in range(count)]
    return lax.ppermute(value, axis, pairs)


def with_halo(array, sides, width, wrap):
    for axis, dim in sides:
        count, length = (lax.axis_size(axis), array.shape[dim])
        up = [(i, (i + 1) % count) for i in range(count if wrap else count - 1)]
        down = [(j, i) for i, j in up]
        last = lax.slice_in_dim(array, length - width, length, axis=dim)
        initial = lax.slice_in_dim(array, 0, width, axis=dim)
        before = lax.ppermute(last, axis, up)
        after = lax.ppermute(initial, axis, down)
        array = jnp.concatenate([before, array, after], axis=dim)
    return array


def basis_filters():
    radius = KSIZE // 2
    centred = jnp.arange(KSIZE, dtype=jnp.float32) - radius
    along_x = []
    along_y = []
    for spread in SPREADS:
        gaussian = jnp.exp(-(centred * centred) / (2.0 * spread * spread))
        scaled = centred / spread
        for power_x in range(5):
            for power_y in range(5 - power_x):
                filter_x = gaussian * scaled**power_x
                filter_y = gaussian * scaled**power_y
                along_x.append(filter_x / jnp.sum(jnp.abs(filter_x)))
                along_y.append(filter_y / jnp.sum(jnp.abs(filter_y)))
    return (jnp.stack(along_y, 1), jnp.stack(along_x, 1))


def psf_kernel(coefs, along_y, along_x):
    return jnp.dot(
        along_y * coefs[None, :],
        along_x.T,
        precision=lax.Precision.HIGHEST,
        preferred_element_type=jnp.float32,
    )


def match_direct(exposure, kernel):
    radius = KSIZE // 2
    extent = exposure.shape[0]
    padded = jnp.pad(exposure, radius)
    row_sums = jnp.zeros((KSIZE, extent + 2 * radius, extent), jnp.float32)
    for tap_index in range(KSIZE):
        row_sums = (
            row_sums
            + kernel[:, tap_index][:, None, None] * padded[None, :, tap_index : tap_index + extent]
        )
    result = jnp.zeros((extent, extent), jnp.float32)
    for tap_index in range(KSIZE):
        result = result + row_sums[tap_index, tap_index : tap_index + extent, :]
    return result


def place_one(tile_one, corner):
    margin = PATCH - TILE
    strip = jnp.pad(tile_one, ((margin, margin), (margin, margin)))
    start_row = (margin - corner[0]).astype(jnp.int32)
    start_col = (margin - corner[1]).astype(jnp.int32)
    return lax.dynamic_slice(strip, (start_row, start_col), (PATCH, PATCH))


def placed_all(tiles, corners):
    return jax.vmap(place_one)(tiles, corners)


def place_tiles(canvases, numer_tiles, denom_tiles, corners):
    count = numer_tiles.shape[0]
    block = min(16, count)
    while count % block != 0:
        block = block - 1
    group_count = count // block
    numer_groups = numer_tiles.reshape(group_count, block, TILE, TILE)
    denom_groups = denom_tiles.reshape(group_count, block, TILE, TILE)
    corner_groups = corners.reshape(group_count, block, 2)

    def step_group(totals, entry):
        numer_all, denom_all = totals
        group_num, group_den, group_corner = entry
        numer_all = numer_all + jnp.sum(placed_all(group_num, group_corner), 0)
        denom_all = denom_all + jnp.sum(placed_all(group_den, group_corner), 0)
        return ((numer_all, denom_all), None)

    totals, ignored = lax.scan(step_group, canvases, (numer_groups, denom_groups, corner_groups))
    return totals


def on_device(
    exposures, variance, coef_table, coef_index, offsets, tile_codes, detect_ra, detect_dec
):
    owners = lax.axis_size("src")
    code_total = 2 * owners
    slot_total = code_total * CAP
    local_tiles = exposures[0]
    local_var = variance[0]
    codes_here = tile_codes[0]
    corners = offsets[0]
    tile_count = local_tiles.shape[0]
    along_y, along_x = basis_filters()
    picks = (
        coef_index[0][:, None] == jnp.arange(coef_table.shape[0], dtype=jnp.int32)[None, :]
    ).astype(jnp.float32)
    coefs = jnp.dot(
        picks, coef_table, precision=lax.Precision.HIGHEST, preferred_element_type=jnp.float32
    )
    kernels = jax.vmap(lambda row_coef: psf_kernel(row_coef, along_y, along_x))(coefs)
    matched = lax.map(lambda pair_in: match_direct(pair_in[0], pair_in[1]), (local_tiles, kernels))
    weight_map = 1.0 / local_var
    weighted = weight_map * matched
    zero_canvas = jnp.zeros((PATCH, PATCH), jnp.float32)
    membership = (codes_here[:, None] == jnp.arange(code_total, dtype=jnp.int32)[None, :]).astype(
        jnp.int32
    )
    earlier = jnp.cumsum(membership, 0) - membership
    rank_here = jnp.sum(earlier * membership, 1)
    slot_of = codes_here * CAP + rank_here
    chooser = (slot_of[None, :] == jnp.arange(slot_total, dtype=jnp.int32)[:, None]).astype(
        jnp.int32
    )
    source = jnp.sum(chooser * jnp.arange(tile_count, dtype=jnp.int32)[None, :], 1)
    filled = jnp.sum(chooser, 1)
    fill_float = filled.astype(jnp.float32)[:, None, None]
    send_num = (jnp.take(weighted, source, 0) * fill_float).reshape(2, owners, CAP, TILE, TILE)
    send_den = (jnp.take(weight_map, source, 0) * fill_float).reshape(2, owners, CAP, TILE, TILE)
    send_corner = (jnp.take(corners, source, 0) * filled[:, None]).reshape(2, owners, CAP, 2)
    got_num, got_den, got_corner = (
        lax.all_to_all(send_num, "src", split_axis=1, concat_axis=1, tiled=True),
        lax.all_to_all(send_den, "src", split_axis=1, concat_axis=1, tiled=True),
        lax.all_to_all(send_corner, "src", split_axis=1, concat_axis=1, tiled=True),
    )
    own_num = got_num[0].reshape(-1, TILE, TILE)
    own_den = got_den[0].reshape(-1, TILE, TILE)
    own_corner = got_corner[0].reshape(-1, 2)
    moved_num, moved_den, moved_corner = from_behind(
        (got_num[1], got_den[1], got_corner[1]), "sky", 1
    )
    all_num = jnp.concatenate([own_num, moved_num.reshape(-1, TILE, TILE)], 0)
    all_den = jnp.concatenate([own_den, moved_den.reshape(-1, TILE, TILE)], 0)
    all_corner = jnp.concatenate([own_corner, moved_corner.reshape(-1, 2)], 0)
    numerator, denominator = place_tiles((zero_canvas, zero_canvas), all_num, all_den, all_corner)
    coadd = numerator / (denominator + 1.0)
    extended = with_halo(coadd, (("src", 1),), RIM, False)
    filtered = jnp.zeros_like(coadd)
    for tap_index in range(DSIZE):
        filtered = filtered + detect_dec[tap_index] * extended[:, tap_index : tap_index + PATCH]
    wrapped = with_halo(filtered, (("sky", 0),), RIM, True)
    detection = jnp.zeros_like(coadd)
    for tap_index in range(DSIZE):
        detection = detection + detect_ra[tap_index] * wrapped[tap_index : tap_index + PATCH]
    return (coadd, detection)


def solution(mesh):
    return jax.shard_map(
        on_device,
        mesh=mesh,
        in_specs=(
            P("sky", "src", None, None),
            P("sky", "src", None, None),
            P(),
            P("sky", "src"),
            P("sky", "src", None),
            P("sky", "src"),
            P(),
            P(),
        ),
        out_specs=(P("sky", "src"), P("sky", "src")),
        check_vma=False,
    )
```

profile of v0, /device:TPU:1, one launch (start us, length us, event | category | flops | bytes accessed | tf_op | source)
XLA Modules:
  0.0 1146.6 jit_solution(1416983545050628289)
XLA Ops:
  24.7 216.7 %while.34 = (s32[]{:T(128)}, f32[16,256,256]{2,1,0:T(8,128)}, f32[16,21,21]{1,2,0:T(8,128)S(1)}, f32[16,256,256]{2,1,0:T(8,128)}, s32[]{:T(128)}) while((s32[]{:T(128)}, f32[16,256,256]{2,1,0:T(8,128)}, f32[16,21,21]{1,2,0:T(8,128)S(1)}, f32[16,256,256]{2,1,0:T(8,128)}, s32[]{:T(128)}) %tuple.268), condition=%wide.region_16.0_spmd, body=%wide.region_15.0_spmd.sunk | while | flops 62145536 | bytes 24630456 | solution.py:130
  54.4 9.6 multiply_add_fusion.2
  68.0 9.6 multiply_add_fusion.2
  81.5 9.6 multiply_add_fusion.2
  95.1 9.6 multiply_add_fusion.2
  108.6 9.6 multiply_add_fusion.2
  122.1 9.6 multiply_add_fusion.2
  203.4 9.6 multiply_add_fusion.2
  216.9 9.6 multiply_add_fusion.2
  264.1 9.8 select_multiply_fusion
  291.4 86.3 %all-to-all-done.2 = f32[2,8,2,256,256]{4,3,2,0,1:T(8,128)} async-done(((f32[2,8,2,256,256]{4,3,2,0,1:T(8,128)}), f32[2,8,2,256,256]{4,3,2,0,1:T(8,128)}, u32[]{:S(2)}, u32[]{:S(2)}) %all-to-all-start.2) | async-done | bytes 8388640 | tf_op jit(solution)/shard_map/all_to_all | solution.py:151
  392.5 84.8 %all-to-all-done = f32[2,8,2,256,256]{4,3,2,0,1:T(8,128)} async-done(((f32[2,8,2,256,256]{4,3,2,0,1:T(8,128)}), f32[2,8,2,256,256]{4,3,2,0,1:T(8,128)}, u32[]{:S(2)}, u32[]{:S(2)}) %all-to-all-start) | async-done | bytes 8388640 | tf_op jit(solution)/shard_map/all_to_all | solution.py:150
  498.5 82.8 %collective-permute-done.1 = s32[8,2,2]{0,2,1:T(2,128)S(1)} collective-permute-done((s32[8,2,2]{0,2,1:T(2,128)S(1)}, s32[8,2,2]{0,2,1:T(2,128)S(1)}, u32[]{:S(2)}, u32[]{:S(2)}) %collective-permute-start.1) | collective-permute-done | bytes 160 | tf_op jit(solution)/shard_map/ppermute | solution.py:20
  596.1 457.3 %while.37 = (s32[]{:T(128)}, f32[512,512]{1,0:T(8,128)S(1)}, f32[512,512]{1,0:T(8,128)S(1)}, f32[2,16,256,256]{3,2,1,0:T(8,128)}, s32[2,16,2]{1,0,2:T(2,128)S(1)...) while((s32[]{:T(128)}, f32[512,512]{1,0:T(8,128)S(1)}, ...), condition=%wide.region_24.26_spmd.clone, body=%wide.region_21.25_spmd.clone.sunk | while | flops 8913127 | bytes 180360624 | solution.py:107
  602.4 12.4 %pad.1022 = f32[16,768,768]{2,1,0:T(8,128)} pad(f32[16,256,256]{2,1,0:T(8,128)S(1)} %get-tuple-element.675, f32[]{:T(128)} %constant.113.clone.4..sunk), padding=0_0x256_256x256_256 | pad | bytes 41943044 | tf_op jit(solution)/shard_map/while/body/eval_jaxpr/vmap(jit(_pad))/pad | solution.py:80
  622.7 81.8 %while.39 = (s32[]{:T(128)}, f32[16,768,768]{2,1,0:T(8,128)}, s32[16,3]{0,1:T(4,128)S(1)}, f32[16,512,512]{2,1,0:T(8,128)}, s32[]{:T(128)}) while((s32[]{:T(128)}, f32[16,768,768]{2,1,0:T(8,128)}, s32[16,3]{0,1:T(4,128)S(1)}, f32[16,512,512]{2,1,0:T(8,128)}, s32[]{:T(128)}) %tuple.256), condition=%wide.while_cond.1, body=%wide.while_body.1.sunk | while | flops 2 | bytes 2099313 | solution.py:83
  712.9 14.0 %pad.1021 = f32[16,768,768]{2,1,0:T(8,128)} pad(f32[16,256,256]{2,1,0:T(8,128)} %get-tuple-element.671, f32[]{:T(128)} %constant.113.clone.4..sunk), padding=0_0x256_256x256_256 | pad | bytes 41943044 | tf_op jit(solution)/shard_map/while/body/eval_jaxpr/vmap(jit(_pad))/pad | solution.py:80
  734.8 81.7 %while.38 = (s32[]{:T(128)}, f32[16,768,768]{2,1,0:T(8,128)}, s32[16,3]{0,1:T(4,128)S(1)}, f32[16,512,512]{2,1,0:T(8,128)}, s32[]{:T(128)}) while((s32[]{:T(128)}, f32[16,768,768]{2,1,0:T(8,128)}, s32[16,3]{0,1:T(4,128)S(1)}, f32[16,512,512]{2,1,0:T(8,128)}, s32[]{:T(128)}) %tuple.267), condition=%wide.while_cond, body=%wide.while_body.sunk | while | flops 2 | bytes 2099313 | solution.py:83
  831.0 12.4 %pad.1022 = f32[16,768,768]{2,1,0:T(8,128)} pad(f32[16,256,256]{2,1,0:T(8,128)S(1)} %get-tuple-element.675, f32[]{:T(128)} %constant.113.clone.4..sunk), padding=0_0x256_256x256_256 | pad | bytes 41943044 | tf_op jit(solution)/shard_map/while/body/eval_jaxpr/vmap(jit(_pad))/pad | solution.py:80
  851.3 81.8 %while.39 = (s32[]{:T(128)}, f32[16,768,768]{2,1,0:T(8,128)}, s32[16,3]{0,1:T(4,128)S(1)}, f32[16,512,512]{2,1,0:T(8,128)}, s32[]{:T(128)}) while((s32[]{:T(128)}, f32[16,768,768]{2,1,0:T(8,128)}, s32[16,3]{0,1:T(4,128)S(1)}, f32[16,512,512]{2,1,0:T(8,128)}, s32[]{:T(128)}) %tuple.256), condition=%wide.while_cond.1, body=%wide.while_body.1.sunk | while | flops 2 | bytes 2099313 | solution.py:83
  941.5 14.0 %pad.1021 = f32[16,768,768]{2,1,0:T(8,128)} pad(f32[16,256,256]{2,1,0:T(8,128)} %get-tuple-element.671, f32[]{:T(128)} %constant.113.clone.4..sunk), padding=0_0x256_256x256_256 | pad | bytes 41943044 | tf_op jit(solution)/shard_map/while/body/eval_jaxpr/vmap(jit(_pad))/pad | solution.py:80
  963.4 81.7 %while.38 = (s32[]{:T(128)}, f32[16,768,768]{2,1,0:T(8,128)}, s32[16,3]{0,1:T(4,128)S(1)}, f32[16,512,512]{2,1,0:T(8,128)}, s32[]{:T(128)}) while((s32[]{:T(128)}, f32[16,768,768]{2,1,0:T(8,128)}, s32[16,3]{0,1:T(4,128)S(1)}, f32[16,512,512]{2,1,0:T(8,128)}, s32[]{:T(128)}) %tuple.267), condition=%wide.while_cond, body=%wide.while_body.sunk | while | flops 2 | bytes 2099313 | solution.py:83
  1064.6 42.7 %fusion.4 = f32[512,512]{1,0:T(8,128)S(1)} fusion(f32[512,512]{1,0:T(8,128)S(1)} %add_divide_fusion, f32[512,20]{1,0:T(8,128)S(1)} %collective-permute-done.4, f32[512,20]{1,0:T(8,128)S(1)} %collective-permute-done.3, f32[]{:T(128)} %bitcast.86, f32[]{:T(128)} %bitcast.85, f32[]{:T(128)} %bitcast.84, f32[]{:T(128)} %bitcast.83, f32[]{:T(128)} %bitcast.82, ...), kind=kLoop, calls=%fused_computation.205 | loop fusion | flops 31719424 | bytes 2179236 | tf_op jit(solution)/shard_map/add | solution.py:168
  1113.7 32.5 %fusion.120 = f32[512,512]{1,0:T(8,128)} fusion(f32[20,512]{1,0:T(8,128)S(1)} %collective-permute-done.6, f32[20,512]{1,0:T(8,128)S(1)} %collective-permute-done.5, f32[512,512]{1,0:T(8,128)S(1)} %fusion.4, f32[]{:T(128)} %bitcast.126, f32[]{:T(128)} %bitcast.125, f32[]{:T(128)} %bitcast.124, f32[]{:T(128)} %bitcast.123, f32[]{:T(128)} %bitcast.122, ...), kind=kLoop, calls=%fused_computation.321 | loop fusion | flops 31719424 | bytes 2179236 | tf_op jit(solution)/shard_map/add | solution.py:172
  (448 shorter events, 675.6 us)
Async XLA Ops:
  0.6 22.1 %copy-start = (f32[64,45]{0,1:T(8,128)S(1)}, f32[64,45]{0,1:T(8,128)}, u32[]{:S(2)}) copy-start(f32[64,45]{0,1:T(8,128)} %param.16) | copy-start | bytes 34564
  241.4 4.9 copy-start.2
  277.7 100.0 %all-to-all-start.2 = ((f32[2,8,2,256,256]{4,3,2,0,1:T(8,128)}), f32[2,8,2,256,256]{4,3,2,0,1:T(8,128)}, u32[]{:S(2)}, u32[]{:S(2)}) async-start(f32[2,8,2,256,256]{4,3,2,0,1:T(8,128)} %copy.60), calls=%async_computation.2 | async-start | bytes 16777216 | tf_op jit(solution)/shard_map/all_to_all | solution.py:151
  377.7 99.6 %all-to-all-start = ((f32[2,8,2,256,256]{4,3,2,0,1:T(8,128)}), f32[2,8,2,256,256]{4,3,2,0,1:T(8,128)}, u32[]{:S(2)}, u32[]{:S(2)}) async-start(f32[2,8,2,256,256]{4,3,2,0,1:T(8,128)} %copy.53), calls=%async_computation | async-start | bytes 16777216 | tf_op jit(solution)/shard_map/all_to_all | solution.py:150
  391.1 95.3 %copy-start.9 = (s32[1,16,2]{1,2,0:T(2,128)S(1)}, s32[1,16,2]{1,2,0:T(2,128)}, u32[]{:S(2)}) copy-start(s32[1,16,2]{1,2,0:T(2,128)} %param.18) | copy-start | bytes 388
  391.1 101.3 %copy-start.5 = (f32[41]{0:T(128)S(1)}, f32[41]{0:T(128)}, u32[]{:S(2)}) copy-start(f32[41]{0:T(128)} %param.21) | copy-start | bytes 496
  391.1 102.8 %copy-start.7 = (f32[41]{0:T(128)S(1)}, f32[41]{0:T(128)}, u32[]{:S(2)}) copy-start(f32[41]{0:T(128)} %param.20) | copy-start | bytes 496
  391.1 190.6 %collective-permute-start.2 = (f32[8,2,256,256]{3,2,1,0:T(8,128)}, f32[8,2,256,256]{3,2,1,0:T(8,128)}, u32[]{:S(2)}, u32[]{:S(2)}) collective-permute-start(f32[8,2,256,256]{3,2,1,0:T(8,128)} %get-tuple-element.348), channel_id=1, source_target_pairs={{0,8},{8,16},{16,24},{24,32},{32,40},{40,48},{48,56},{56,64},{64,7... | collective-permute-start | bytes 12582920 | tf_op jit(solution)/shard_map/ppermute | solution.py:20
  484.9 104.5 %collective-permute-start = (f32[8,2,256,256]{3,2,1,0:T(8,128)}, f32[8,2,256,256]{3,2,1,0:T(8,128)}, u32[]{:S(2)}, u32[]{:S(2)}) collective-permute-start(f32[8,2,256,256]{3,2,1,0:T(8,128)} %get-tuple-element.350), channel_id=1, source_target_pairs={{0,8},{8,16},{16,24},{24,32},{32,40},{40,48},{48,56},{56,64},{64,7... | collective-permute-start | bytes 12582920 | tf_op jit(solution)/shard_map/ppermute | solution.py:20
  487.9 9.6 all-to-all-start.1
  497.6 83.7 %collective-permute-start.1 = (s32[8,2,2]{0,2,1:T(2,128)S(1)}, s32[8,2,2]{0,2,1:T(2,128)S(1)}, u32[]{:S(2)}, u32[]{:S(2)}) collective-permute-start(s32[8,2,2]{0,2,1:T(2,128)S(1)} %bitcast.218), channel_id=1, source_target_pairs={{0,8},{8,16},{16,24},{24,32},{32,40},{40,48},{48,56},{56,64},{64,7... | collective-permute-start | bytes 392 | tf_op jit(solution)/shard_map/ppermute | solution.py:20
  581.6 7.7 copy-start.3
  596.1 462.9 %copy-start.6 = (f32[41]{0:T(128)S(1)}, f32[41]{0:T(128)}, u32[]{:S(2)}) copy-start(f32[41]{0:T(128)} %param.21) | copy-start | bytes 496
  1053.4 58.7 %copy-start.8 = (f32[41]{0:T(128)S(1)}, f32[41]{0:T(128)}, u32[]{:S(2)}) copy-start(f32[41]{0:T(128)} %param.20) | copy-start | bytes 496
  1053.5 92.7 %copy-start.1 = (f32[64,45]{0,1:T(8,128)S(1)}, f32[64,45]{0,1:T(8,128)}, u32[]{:S(2)}) copy-start(f32[64,45]{0,1:T(8,128)} %param.16) | copy-start | bytes 34564
  1053.7 92.5 %copy-start.4 = (f32[512,512]{1,0:T(8,128)}, f32[512,512]{1,0:T(8,128)S(1)}, u32[]{:S(2)}) copy-start(f32[512,512]{1,0:T(8,128)S(1)} %add_divide_fusion) | copy-start | bytes 3145732
  1053.9 6.3 collective-permute-start.3
  1056.9 7.7 collective-permute-start.4
  1107.3 6.3 collective-permute-start.5
  1107.4 6.2 collective-permute-start.6
where the time goes:
time: 1160 us; the launch traced here: 1150 us
  local copies, waits for them, and re-layouts  513 us (44%)
  other arithmetic  337 us (29%)
  waiting for transfers between devices  262 us (23%)
  starting transfers between devices  30 us (3%)
    gather x192, local copies, waits for them, and re-layouts  327 us
    add x16, other arithmetic, match_direct(): row_sums + kernel[:, tap_index][:, None, None] * padded[None, :, tap_inde...  153 us
    all_to_all x1, waiting for transfers between devices, on_device(): lax.all_to_all(send_den, 'src', split_axis=1, concat_axis=1, tiled=True)  86.3 us
    all_to_all x1, waiting for transfers between devices, on_device(): lax.all_to_all(send_num, 'src', split_axis=1, concat_axis=1, tiled=True)  84.8 us
    ppermute x3, waiting for transfers between devices, from_behind(): return lax.ppermute(value, axis, pairs)  82.8 us
    pad x4, local copies, waits for them, and re-layouts, place_one(): strip = jnp.pad(tile_one, ((margin, margin), (margin, margin)))  52.8 us
    add x1, other arithmetic, on_device(): filtered + detect_dec[tap_index] * extended[:, tap_index:tap_index + PATCH]  42.7 us
    add x1, other arithmetic, on_device(): detection + detect_ra[tap_index] * wrapped[tap_index:tap_index + PATCH]  32.5 us
  transfers between devices with their start and end apart: 10, of which 7 were waited for; matrix products, arithmetic and copies ran while one was open for 3% of the time, Pallas kernels for 0%

commit v1 on v0

v1 whole, which is shorter than its diff:
```python
import functools

import jax
import jax.numpy as jnp
import numpy as np
from jax import lax
from jax.experimental import pallas as pl
from jax.experimental.pallas import tpu as pltpu
from jax.sharding import PartitionSpec as P

TILE = 256
PATCH = 512
KSIZE = 21
DSIZE = 41
RIM = 20
TILES = 16
SLOTS = 16
SPREADS = (0.75, 1.5, 3.0)
F32 = jnp.float32
BF16 = jnp.bfloat16


def basis_filters():
    u = np.arange(KSIZE, dtype=np.float32) - np.float32(KSIZE // 2)
    hx, hy = [], []
    for spread in SPREADS:
        g = np.exp(-(u * u) / np.float32(2.0 * spread * spread)).astype(np.float32)
        scaled = (u / np.float32(spread)).astype(np.float32)
        for p in range(5):
            for q in range(5 - p):
                fx = (g * scaled**p).astype(np.float32)
                fy = (g * scaled**q).astype(np.float32)
                hx.append(fx / np.sum(np.abs(fx)))
                hy.append(fy / np.sum(np.abs(fy)))
    return np.stack(hy, 1).astype(np.float32), np.stack(hx, 1).astype(np.float32)


def split(x):
    hi = x.astype(BF16)
    return hi, (x - hi.astype(F32)).astype(BF16)


def mm(a, b):
    return jnp.dot(a, b, preferred_element_type=F32)


def weights_body(info, codes, offs, v_ref, mine, part, dest, tab_mine, tab_part, buf, cnt, sem):
    n = pl.program_id(0)
    b = n & 1

    @pl.when(n == 0)
    def _():
        def zero(i, _):
            tab_mine[i] = 0
            tab_part[i] = 0
            return 0

        lax.fori_loop(0, 3 * SLOTS, zero, 0)

        def zero_count(i, _):
            cnt[i] = 0
            return 0

        lax.fori_loop(0, 16, zero_count, 0)

    code = codes[n]
    rank = cnt[code]
    cnt[code] = rank + 1
    owner = code & 7
    away = ((owner >> 1) - info[0]) & 3
    par = (owner & 1) ^ info[1]
    slot = (((code >> 3) * 4 + away) * 2) + rank
    dest[n] = par * SLOTS + slot

    @pl.when(n >= 2)
    def _():
        pltpu.make_async_copy(buf.at[b], mine.at[0], sem.at[b]).wait()

    buf[b] = 1.0 / v_ref[0]

    @pl.when(par == 0)
    def _():
        tab_mine[slot * 3] = 1
        tab_mine[slot * 3 + 1] = offs[2 * n]
        tab_mine[slot * 3 + 2] = offs[2 * n + 1]
        pltpu.make_async_copy(buf.at[b], mine.at[slot], sem.at[b]).start()

    @pl.when(par != 0)
    def _():
        tab_part[slot * 3] = 1
        tab_part[slot * 3 + 1] = offs[2 * n]
        tab_part[slot * 3 + 2] = offs[2 * n + 1]
        pltpu.make_async_copy(buf.at[b], part.at[slot], sem.at[b]).start()

    @pl.when(n == TILES - 1)
    def _():
        pltpu.make_async_copy(buf.at[1 - b], mine.at[0], sem.at[1 - b]).wait()
        pltpu.make_async_copy(buf.at[b], mine.at[0], sem.at[b]).wait()


def weights(info, codes, offs, variance):
    slots = jax.ShapeDtypeStruct((SLOTS, TILE, TILE), F32)
    table = jax.ShapeDtypeStruct((3 * SLOTS,), jnp.int32)
    return pl.pallas_call(
        weights_body,
        out_shape=(slots, slots, jax.ShapeDtypeStruct((TILES,), jnp.int32), table, table),
        grid_spec=pltpu.PrefetchScalarGridSpec(
            num_scalar_prefetch=3,
            grid=(TILES,),
            in_specs=[pl.BlockSpec((1, TILE, TILE), lambda n, *_: (n, 0, 0))],
            out_specs=(
                pl.BlockSpec(memory_space=pl.ANY),
                pl.BlockSpec(memory_space=pl.ANY),
                pl.BlockSpec(memory_space=pltpu.SMEM),
                pl.BlockSpec(memory_space=pltpu.SMEM),
                pl.BlockSpec(memory_space=pltpu.SMEM),
            ),
            scratch_shapes=[
                pltpu.VMEM((2, TILE, TILE), F32),
                pltpu.SMEM((16,), jnp.int32),
                pltpu.SemaphoreType.DMA((2,)),
            ],
        ),
        cost_estimate=pl.CostEstimate(flops=1 << 20, bytes_accessed=8 << 20, transcendentals=0),
        name="weights",
    )(info, codes, offs, variance)


def build_rows(g_ref, s, out):
    base = jnp.broadcast_to(g_ref[0, pl.ds(s, 1), :], (16, TILE))
    first = pltpu.roll(base, 0, 1, stride=1, stride_axis=0)
    row = lax.broadcasted_iota(jnp.int32, (16, TILE), 0)
    lane = lax.broadcasted_iota(jnp.int32, (16, TILE), 1)
    for i in range(8):
        band = first if i == 0 else pltpu.roll(first, 16 * i, 1)
        other = jnp.concatenate([band[:, 128:], band[:, :128]], axis=1)
        if i == 0:
            band = jnp.where(lane - row <= 10, band, 0.0)
        if i == 7:
            other = jnp.where(row + 240 - lane <= 10, other, 0.0)
        for at, rows in ((i, band), (i + 8, other)):
            hi, lo = split(rows)
            out[16 * at : 16 * at + 16, :] = hi
            out[TILE + 16 * at : TILE + 16 * at + 16, :] = lo


def match_body(dest, e_ref, v_ref, g_ref, mine, part, both, b0, b1, acc, buf, sem):
    n = pl.program_id(0)
    b = n & 1
    hi, lo = split(e_ref[0])
    both[0:TILE, :] = hi
    both[TILE : 2 * TILE, :] = lo
    acc[...] = jnp.zeros_like(acc)

    def add_rows(w, s):
        two = mm(both[...], w[0:TILE, :])
        sums = two[0:TILE] + two[TILE:] + mm(both[0:TILE, :], w[TILE : 2 * TILE, :])
        low = pl.multiple_of(16 - 8 * (s >> 3), 8)
        acc[s & 7, pl.ds(low, TILE), :] += sums

    build_rows(g_ref, 0, b0)

    def pair(i, _):
        s = 2 * i
        build_rows(g_ref, s + 1, b1)
        add_rows(b0, s)
        build_rows(g_ref, s + 2, b0)
        add_rows(b1, s + 1)
        return 0

    lax.fori_loop(0, 10, pair, 0)
    add_rows(b0, jnp.int32(20))

    matched = acc[0, 6 : 6 + TILE, :]
    for r in range(1, 8):
        matched = matched + acc[r, r + 6 : r + 6 + TILE, :]

    @pl.when(n >= 2)
    def _():
        pltpu.make_async_copy(buf.at[b], mine.at[0], sem.at[b]).wait()

    buf[b] = matched * (1.0 / v_ref[0])
    where = dest[n]

    @pl.when(where < SLOTS)
    def _():
        pltpu.make_async_copy(buf.at[b], mine.at[where], sem.at[b]).start()

    @pl.when(where >= SLOTS)
    def _():
        pltpu.make_async_copy(buf.at[b], part.at[where - SLOTS], sem.at[b]).start()

    @pl.when(n == TILES - 1)
    def _():
        pltpu.make_async_copy(buf.at[1 - b], mine.at[0], sem.at[1 - b]).wait()
        pltpu.make_async_copy(buf.at[b], mine.at[0], sem.at[b]).wait()


def match(dest, exposures, variance, rows):
    slots = jax.ShapeDtypeStruct((SLOTS, TILE, TILE), F32)
    tile = pl.BlockSpec((1, TILE, TILE), lambda n, *_: (n, 0, 0))
    return pl.pallas_call(
        match_body,
        out_shape=(slots, slots),
        grid_spec=pltpu.PrefetchScalarGridSpec(
            num_scalar_prefetch=1,
            grid=(TILES,),
            in_specs=[tile, tile, pl.BlockSpec((1, 24, TILE), lambda n, *_: (n, 0, 0))],
            out_specs=(pl.BlockSpec(memory_space=pl.ANY), pl.BlockSpec(memory_space=pl.ANY)),
            scratch_shapes=[
                pltpu.VMEM((2 * TILE, TILE), BF16),
                pltpu.VMEM((2 * TILE, TILE), BF16),
                pltpu.VMEM((2 * TILE, TILE), BF16),
                pltpu.VMEM((8, TILE + 16, TILE), F32),
                pltpu.VMEM((2, TILE, TILE), F32),
                pltpu.SemaphoreType.DMA((2,)),
            ],
        ),
        cost_estimate=pl.CostEstimate(
            flops=16 * 63 * 2 * 256**3, bytes_accessed=12 << 20, transcendentals=0
        ),
        name="match",
    )(dest, exposures, variance, rows)


def place(canvas, tile_ref, k, r, c):
    rq, rr, cq, cr = r >> 3, r & 7, c >> 7, c & 127
    columns = pl.ds(pl.multiple_of(cq * 128, 128), 384)
    keep_lane = lax.broadcasted_iota(jnp.int32, (64, 128), 1) >= cr
    keep_row = lax.broadcasted_iota(jnp.int32, (8, 8, 384), 1) >= rr
    carry = jnp.zeros((1, 8, 384), F32)
    for chunk in range(4):
        rows = slice(64 * chunk, 64 * chunk + 64)
        left = pltpu.roll(tile_ref[k, rows, 0:128], cr, 1)
        right = pltpu.roll(tile_ref[k, rows, 128:256], cr, 1)
        wide = jnp.concatenate(
            [
                jnp.where(keep_lane, left, 0.0),
                jnp.where(keep_lane, right, left),
                jnp.where(keep_lane, 0.0, right),
            ],
            axis=1,
        )
        turned = pltpu.roll(wide.reshape(8, 8, 384), rr, 1)
        above = jnp.concatenate([carry, turned[:7]], axis=0)
        canvas[pl.ds(rq + 8 * chunk, 8), :, columns] += jnp.where(keep_row, turned, above)
        carry = turned[7:8]
    canvas[pl.ds(rq + 32, 1), :, columns] += jnp.where(keep_row[0:1], 0.0, carry)


def gather_body(row, tab_mine, tab_other, mine, other, keep, plus, minus, hold, canvas):
    away = pl.program_id(0)
    canvas[...] = jnp.zeros_like(canvas)
    for table, ref in ((tab_mine, mine), (tab_other, other)):
        for k in range(2):
            at = ((row * 4 + away) * 2 + k) * 3

            @pl.when(table[at] == 1)
            def _():
                place(canvas, ref, k, table[at + 1], table[at + 2])

    def top():
        return canvas[0:32, :, 0:PATCH].reshape(TILE, PATCH)

    def bottom():
        return canvas[32:64, :, 0:PATCH].reshape(TILE, PATCH)

    @pl.when(away == 0)
    def _():
        keep[0] = top()
        keep[1] = bottom()

    @pl.when(away == 1)
    def _():
        hold[0] = top()
        plus[1] = bottom()

    @pl.when(away == 2)
    def _():
        plus[0] = top()
        minus[0] = bottom()

    @pl.when(away == 3)
    def _():
        minus[1] = top()
        hold[1] = bottom()


def gather(row, tab_mine, tab_other, mine, other):
    halves = jax.ShapeDtypeStruct((2, TILE, PATCH), F32)
    whole = pl.BlockSpec((2, TILE, PATCH), lambda d, *_: (0, 0, 0))
    pair = pl.BlockSpec((2, TILE, TILE), lambda d, *_: (row * 4 + d, 0, 0))
    return pl.pallas_call(
        functools.partial(gather_body, row),
        out_shape=(halves,) * 4,
        grid_spec=pltpu.PrefetchScalarGridSpec(
            num_scalar_prefetch=2,
            grid=(4,),
            in_specs=[pair, pair],
            out_specs=(whole,) * 4,
            scratch_shapes=[pltpu.VMEM((65, 8, 640), F32)],
        ),
        cost_estimate=pl.CostEstimate(flops=8 << 20, bytes_accessed=8 << 20, transcendentals=0),
        name="gather",
    )(tab_mine, tab_other, mine, other)


def taps_body(base_ref, out):
    base = jnp.broadcast_to(base_ref[0], (64, PATCH))
    first = pltpu.roll(base, 0, 1, stride=1, stride_axis=0)
    for i in range(8):
        band = first if i == 0 else pltpu.roll(first, 64 * i, 1)
        hi, lo = split(band)
        out[0, 0, 64 * i : 64 * i + 64, :] = hi
        out[0, 1, 64 * i : 64 * i + 64, :] = lo


def tap_matrices(bases):
    return pl.pallas_call(
        taps_body,
        out_shape=jax.ShapeDtypeStruct((2, 2, PATCH, PATCH), BF16),
        grid=(2,),
        in_specs=[pl.BlockSpec((1, 1, PATCH), lambda i: (i, 0, 0))],
        out_specs=pl.BlockSpec((1, 2, PATCH, PATCH), lambda i: (i, 0, 0, 0)),
        name="taps",
    )(bases)


def near(shape, row0, col0):
    row = lax.broadcasted_iota(jnp.int32, shape, 0) + row0
    col = lax.broadcasted_iota(jnp.int32, shape, 1) + col0
    return jnp.abs(row - col) <= RIM


def dot3(a_hi, a_lo, b_hi, b_lo):
    return mm(a_hi, b_hi) + mm(a_lo, b_hi) + mm(a_hi, b_lo)


def columns_body(c_ref, left, right, t_ref, out):
    inside = near((PATCH, PATCH), 0, 0)
    zero = jnp.zeros((), BF16)
    t_hi, t_lo = t_ref[0, 0], t_ref[0, 1]
    c_hi, c_lo = split(c_ref[...])
    out[...] = dot3(c_hi, c_lo, jnp.where(inside, t_hi, zero), jnp.where(inside, t_lo, zero))
    l_hi, l_lo = split(left[...])
    out[:, 0:128] += dot3(l_hi, l_lo, t_hi[384:, 0:128], t_lo[384:, 0:128])
    r_hi, r_lo = split(right[...])
    out[:, 384:] += dot3(r_hi, r_lo, t_hi[0:128, 384:], t_lo[0:128, 384:])


def rows_body(f_ref, above, below, t_ref, out, pad):
    inside = near((PATCH, PATCH), 0, 0)
    zero = jnp.zeros((), BF16)
    t_hi, t_lo = t_ref[0, 0], t_ref[0, 1]
    f_hi, f_lo = split(f_ref[...])
    out[...] = dot3(jnp.where(inside, t_hi, zero), jnp.where(inside, t_lo, zero), f_hi, f_lo)
    pad[...] = jnp.zeros_like(pad)
    pad[104:128, :] = above[...]
    a_hi, a_lo = split(pad[...])
    out[0:128, :] += dot3(t_hi[0:128, 384:], t_lo[0:128, 384:], a_hi, a_lo)
    pad[104:128, :] = jnp.zeros((24, PATCH), F32)
    pad[0:24, :] = below[...]
    b_hi, b_lo = split(pad[...])
    out[384:, :] += dot3(t_hi[384:, 0:128], t_lo[384:, 0:128], b_hi, b_lo)


def filter_columns(coadd, left, right, mats):
    return pl.pallas_call(
        columns_body,
        out_shape=jax.ShapeDtypeStruct((PATCH, PATCH), F32),
        grid=(1,),
        in_specs=[
            pl.BlockSpec((PATCH, PATCH), lambda i: (0, 0)),
            pl.BlockSpec((PATCH, 128), lambda i: (0, 0)),
            pl.BlockSpec((PATCH, 128), lambda i: (0, 0)),
            pl.BlockSpec((1, 2, PATCH, PATCH), lambda i: (0, 0, 0, 0)),
        ],
        out_specs=pl.BlockSpec((PATCH, PATCH), lambda i: (0, 0)),
        name="columns",
    )(coadd, left, right, mats)


def filter_rows(filtered, above, below, mats):
    return pl.pallas_call(
        rows_body,
        out_shape=jax.ShapeDtypeStruct((PATCH, PATCH), F32),
        grid=(1,),
        in_specs=[
            pl.BlockSpec((PATCH, PATCH), lambda i: (0, 0)),
            pl.BlockSpec((24, PATCH), lambda i: (0, 0)),
            pl.BlockSpec((24, PATCH), lambda i: (0, 0)),
            pl.BlockSpec((1, 2, PATCH, PATCH), lambda i: (1, 0, 0, 0)),
        ],
        out_specs=pl.BlockSpec((PATCH, PATCH), lambda i: (0, 0)),
        scratch_shapes=[pltpu.VMEM((128, PATCH), F32)],
        name="rows",
    )(filtered, above, below, mats)


def along(value, axis, steps, wrap=True):
    count = lax.axis_size(axis)
    pairs = [(i, (i + steps) % count) for i in range(count) if wrap or 0 <= i + steps < count]
    return lax.ppermute(value, axis, pairs)


def partner(value):
    return lax.ppermute(value, "src", [(i, i ^ 1) for i in range(lax.axis_size("src"))])


def reduce_ring(parts):
    keep, plus, minus, hold = parts
    got_plus = along(plus, "src", 2)
    got_minus = along(minus, "src", -2)
    on_plus = along(hold[0] + got_plus[0], "src", 2)
    on_minus = along(hold[1] + got_minus[0], "src", -2)
    top = keep[0] + on_plus + got_minus[1]
    bottom = keep[1] + got_plus[1] + on_minus
    return jnp.stack([top, bottom])


def on_device(
    exposures, variance, coef_table, coef_index, offsets, tile_codes, detect_ra, detect_dec
):
    me = lax.axis_index("src")
    info = jnp.stack([me >> 1, me & 1]).astype(jnp.int32)
    mine_w, part_w, dest, tab_mine, tab_part = weights(
        info, tile_codes[0], offsets[0].reshape(-1), variance[0]
    )
    tab_other = partner(tab_part)
    other_w = partner(part_w)

    along_y, along_x = basis_filters()
    turned = np.zeros((along_x.shape[1], TILE), np.float32)
    for lag in range(-10, 11):
        turned[:, lag % TILE] = along_x[10 - lag, :]
    picks = (coef_index[0][:, None] == jnp.arange(coef_table.shape[0])[None, :]).astype(F32)
    coefs = jnp.dot(picks, coef_table, precision=lax.Precision.HIGHEST)
    tall = np.concatenate([along_y, np.zeros((3, along_y.shape[1]), np.float32)])
    scaled = (jnp.asarray(tall)[None] * coefs[:, None, :]).reshape(TILES * 24, -1)
    rows = jnp.dot(scaled, jnp.asarray(turned), precision=lax.Precision.HIGHEST)
    rows = rows.reshape(TILES, 24, TILE)

    flip = detect_dec[::-1]
    gap = jnp.zeros((PATCH - DSIZE,), F32)
    bases = jnp.stack(
        [
            jnp.concatenate([flip[RIM:], gap, flip[:RIM]]),
            jnp.concatenate([detect_ra[RIM:], gap, detect_ra[:RIM]]),
        ]
    )[:, None, :]
    mats = tap_matrices(bases)

    den_next = gather(1, tab_mine, tab_other, mine_w, other_w)
    den_here = gather(0, tab_mine, tab_other, mine_w, other_w)
    mine_n, part_n = match(dest, exposures[0], variance[0], rows)
    other_n = partner(part_n)
    den1 = reduce_ring(den_next)
    den0 = reduce_ring(den_here)
    num_next = gather(1, tab_mine, tab_other, mine_n, other_n)
    num_here = gather(0, tab_mine, tab_other, mine_n, other_n)
    num1 = reduce_ring(num_next)
    num0 = reduce_ring(num_here)
    den = den0 + along(den1, "sky", 1)
    num = num0 + along(num1, "sky", 1)
    coadd = (num / (den + 1.0)).reshape(PATCH, PATCH)
    left = along(coadd[:, PATCH - 128 :], "src", 1, wrap=False)
    right = along(coadd[:, :128], "src", -1, wrap=False)
    filtered = filter_columns(coadd, left, right, mats)
    above = along(filtered[PATCH - 24 :], "sky", 1)
    below = along(filtered[:24], "sky", -1)
    detection = filter_rows(filtered, above, below, mats)
    return coadd, detection


def solution(mesh):
    return jax.shard_map(
        on_device,
        mesh=mesh,
        in_specs=(
            P("sky", "src", None, None),
            P("sky", "src", None, None),
            P(),
            P("sky", "src"),
            P("sky", "src", None),
            P("sky", "src"),
            P(),
            P(),
        ),
        out_specs=(P("sky", "src"), P("sky", "src")),
        check_vma=False,
    )
```

time: 1160 us -> 326 us (0.28); the launches traced: 1150 us -> 325 us
  local copies, waits for them, and re-layouts: 513 us -> 5.74 us
  other arithmetic: 337 us -> 11.3 us
  Pallas kernels: 0 us -> 144 us
  waiting for transfers between devices: 262 us -> 128 us
    gather x196 -> x0, local copies, waits for them, and re-layouts: 341 us -> none
    add x22 -> x4, other arithmetic: 230 us -> 5.25 us  [reduce_ring(): on_plus = along(hold[0] + got_plus[0], 'src', 2)]
    all_to_all x3 -> x0, waiting for transfers between devices: 173 us -> none  [the longest x1 86.3 us: on_device(): lax.all_to_all(send_den, 'src', split_axis=1, concat_axis=1, tiled=True)]
    pallas_call x0 -> x9, Pallas kernels: none -> 144 us  [the longest x1 96.6 us: match(): pl.pallas_call(match_body, out_shape=(slots, slots), grid_spec=pltpu.Pref...]
    pad x4 -> x0, local copies, waits for them, and re-layouts: 52.8 us -> none  [place_one(): strip = jnp.pad(tile_one, ((margin, margin), (margin, margin)))]
    slice x45 -> x6, local copies, waits for them, and re-layouts: 47.1 us -> 1.2 us  [the longest x1 0.83 us: on_device(): below = along(filtered[:24], 'sky', -1)]
    reduce_sum x21 -> x0, other arithmetic: 42.5 us -> none  [the longest x2 15.9 us: step_group(): numer_all = numer_all + jnp.sum(placed_all(group_num, group_corner), 0)]
    ppermute x7 -> x25, waiting for transfers between devices: 88.5 us -> 128 us  [the longest x22 121 us: along(): return lax.ppermute(value, axis, pairs)]
  transfers between devices with their start and end apart: 10 -> 25, of which waited for: 7 -> 13; matrix products, arithmetic and copies ran while one was open for 3% -> 4% of each run, Pallas kernels for 0% -> 38%
where the time goes in v1:
time: 326 us; the launch traced here: 325 us
  Pallas kernels  144 us (44%)
  waiting for transfers between devices  128 us (39%)
  starting transfers between devices  33.7 us (10%)
  other arithmetic  11.3 us (3%)
  local copies, waits for them, and re-layouts  5.74 us (2%)
    ppermute x22, waiting for transfers between devices, along(): return lax.ppermute(value, axis, pairs)  121 us
    pallas_call x1, Pallas kernels, match(): pl.pallas_call(match_body, out_shape=(slots, slots), grid_spec=pltpu.Pref...  96.6 us
    ppermute x22, starting transfers between devices, along(): return lax.ppermute(value, axis, pairs)  31.6 us
    pallas_call x4, Pallas kernels, gather(): pl.pallas_call(functools.partial(gather_body, row), out_shape=(halves,) *...  25.8 us
    pallas_call x1, Pallas kernels, weights(): pl.pallas_call(weights_body, out_shape=(slots, slots, jax.ShapeDtypeStruc...  11.5 us
    ppermute x3, waiting for transfers between devices, partner(): lax.ppermute(value, 'src', [(i, i ^ 1) for i in range(lax.axis_size('src'...  6.99 us
  transfers between devices with their start and end apart: 25, of which 13 were waited for; matrix products, arithmetic and copies ran while one was open for 4% of the time, Pallas kernels for 38%

profile of v1, /device:TPU:1, one launch (start us, length us, event | category | flops | bytes accessed | tf_op | source)
XLA Modules:
  0.0 325.0 jit_solution(1022181712636477308)
XLA Ops:
  2.7 11.5 %weights.1 = (f32[16,256,256]{2,1,0:T(8,128)}, f32[16,256,256]{2,1,0:T(8,128)}, s32[16]{0:T(128)}, s32[48]{0:T(128)}, s32[48]{0:T(128)}) custom-call(s32[2]{0:T(128)} %pad_add_fusion.info, s32[16]{0:T(128)} %bitcast.117, s32[32]{0:T(128)} %reshape_squeeze.3.offs, f32[16,256,256]{2,1,0:T(8,128)} %bitcast.113), custom_call_target="tpu_custom_call" | custom-call | flops 1048576 | bytes 8388608 | tf_op jit(solution)/shard_map/weights/pallas_call | solution.py:104
  17.1 96.6 %match.1 = (f32[16,256,256]{2,1,0:T(8,128)}, f32[16,256,256]{2,1,0:T(8,128)}) custom-call(s32[16]{0:T(128)} %get-tuple-element.27.dest, f32[16,256,256]{2,1,0:T(8,128)} %bitcast.119, f32[16,256,256]{2,1,0:T(8,128)} %bitcast.114, f32[16,24,256]{2,1,0:T(8,128)} %fusion.30.g_ref), custom_call_target="tpu_custom_call" | custom-call | flops 33822867456 | bytes 12582912 | tf_op jit(solution)/shard_map/match/pallas_call | solution.py:202
  114.3 7.0 %collective-permute-done.tab_other = s32[48]{0:T(128)S(1)} collective-permute-done((s32[48]{0:T(128)S(1)}, s32[48]{0:T(128)S(1)}, u32[]{:S(2)}, u32[]{:S(2)}) %collective-permute-start) | collective-permute-done | bytes 224 | tf_op jit(solution)/shard_map/ppermute | solution.py:407
  121.8 6.6 %gather.7 = (f32[2,256,512]{2,1,0:T(8,128)}, f32[2,256,512]{2,1,0:T(8,128)}, f32[2,256,512]{2,1,0:T(8,128)}, f32[2,256,512]{2,1,0:T(8,128)}) custom-call(s32[48]{0:T(128)} %get-tuple-element.25.tab_mine, s32[48]{0:T(128)} %copy-done.19, f32[16,256,256]{2,1,0:T(8,128)} %get-tuple-element.38.mine, f32[16,256,256]{2,1,0:T(8,128)} %collective-permute-done.11.other), custom_call_target="tpu_custom_call" | custom-call | flops 8388608 | bytes 8388608 | tf_op jit(solution)/shard_map/gather/pallas_call | solution.py:293
  131.1 6.6 %gather.5 = (f32[2,256,512]{2,1,0:T(8,128)}, f32[2,256,512]{2,1,0:T(8,128)}, f32[2,256,512]{2,1,0:T(8,128)}, f32[2,256,512]{2,1,0:T(8,128)}) custom-call(s32[48]{0:T(128)} %get-tuple-element.25.tab_mine, s32[48]{0:T(128)} %copy-done.19, f32[16,256,256]{2,1,0:T(8,128)} %get-tuple-element.28.mine, f32[16,256,256]{2,1,0:T(8,128)} %collective-permute-done.1.other), custom_call_target="tpu_custom_call" | custom-call | flops 8388608 | bytes 8388608 | tf_op jit(solution)/shard_map/gather/pallas_call | solution.py:293
  137.9 2.4 collective-permute-start.8
  140.3 6.4 %gather.6 = (f32[2,256,512]{2,1,0:T(8,128)}, f32[2,256,512]{2,1,0:T(8,128)}, f32[2,256,512]{2,1,0:T(8,128)}, f32[2,256,512]{2,1,0:T(8,128)}) custom-call(s32[48]{0:T(128)} %get-tuple-element.25.tab_mine, s32[48]{0:T(128)} %copy-done.19, f32[16,256,256]{2,1,0:T(8,128)} %get-tuple-element.38.mine, f32[16,256,256]{2,1,0:T(8,128)} %collective-permute-done.11.other), custom_call_target="tpu_custom_call" | custom-call | flops 8388608 | bytes 8388608 | tf_op jit(solution)/shard_map/gather/pallas_call | solution.py:293
  146.7 7.7 %collective-permute-done.16 = f32[2,256,512]{2,1,0:T(8,128)S(1)} collective-permute-done((f32[2,256,512]{2,1,0:T(8,128)}, f32[2,256,512]{2,1,0:T(8,128)S(1)}, u32[]{:S(2)}, u32[]{:S(2)}) %collective-permute-start.16) | collective-permute-done | bytes 1048608 | tf_op jit(solution)/shard_map/ppermute | solution.py:403
  156.1 2.2 fusion.8
  158.4 6.3 %gather.4 = (f32[2,256,512]{2,1,0:T(8,128)}, f32[2,256,512]{2,1,0:T(8,128)}, f32[2,256,512]{2,1,0:T(8,128)}, f32[2,256,512]{2,1,0:T(8,128)}) custom-call(s32[48]{0:T(128)} %get-tuple-element.25.tab_mine, s32[48]{0:T(128)} %copy-done.19, f32[16,256,256]{2,1,0:T(8,128)} %get-tuple-element.28.mine, f32[16,256,256]{2,1,0:T(8,128)} %collective-permute-done.1.other), custom_call_target="tpu_custom_call" | custom-call | flops 8388608 | bytes 8388608 | tf_op jit(solution)/shard_map/gather/pallas_call | solution.py:293
  164.8 12.2 %collective-permute-done.6 = f32[2,256,512]{2,1,0:T(8,128)} collective-permute-done((f32[2,256,512]{2,1,0:T(8,128)}, f32[2,256,512]{2,1,0:T(8,128)}, u32[]{:S(2)}, u32[]{:S(2)}) %collective-permute-start.6) | collective-permute-done | bytes 1048608 | tf_op jit(solution)/shard_map/ppermute | solution.py:403
  181.1 18.2 %collective-permute-done.12 = f32[2,256,512]{2,1,0:T(8,128)S(1)} collective-permute-done((f32[2,256,512]{2,1,0:T(8,128)}, f32[2,256,512]{2,1,0:T(8,128)S(1)}, u32[]{:S(2)}, u32[]{:S(2)}) %collective-permute-start.12) | collective-permute-done | bytes 1048608 | tf_op jit(solution)/shard_map/ppermute | solution.py:403
  201.0 9.6 %collective-permute-done.17 = f32[256,512]{1,0:T(8,128)} collective-permute-done((f32[256,512]{1,0:T(8,128)}, f32[256,512]{1,0:T(8,128)}, u32[]{:S(2)}, u32[]{:S(2)}) %collective-permute-start.17) | collective-permute-done | bytes 524320 | tf_op jit(solution)/shard_map/ppermute | solution.py:403
  215.3 29.0 %collective-permute-done.7 = f32[256,512]{1,0:T(8,128)S(1)} collective-permute-done((f32[256,512]{1,0:T(8,128)S(1)}, f32[256,512]{1,0:T(8,128)S(1)}, u32[]{:S(2)}, u32[]{:S(2)}) %collective-permute-start.7) | collective-permute-done | bytes 524320 | tf_op jit(solution)/shard_map/ppermute | solution.py:403
  250.6 4.8 %collective-permute-done.13 = f32[256,512]{1,0:T(8,128)S(1)} collective-permute-done((f32[256,512]{1,0:T(8,128)S(1)}, f32[256,512]{1,0:T(8,128)S(1)}, u32[]{:S(2)}, u32[]{:S(2)}) %collective-permute-start.13) | collective-permute-done | bytes 524320 | tf_op jit(solution)/shard_map/ppermute | solution.py:403
  258.5 8.2 %collective-permute-done.3 = f32[256,512]{1,0:T(8,128)S(1)} collective-permute-done((f32[256,512]{1,0:T(8,128)S(1)}, f32[256,512]{1,0:T(8,128)S(1)}, u32[]{:S(2)}, u32[]{:S(2)}) %collective-permute-start.3) | collective-permute-done | bytes 524320 | tf_op jit(solution)/shard_map/ppermute | solution.py:403
  267.7 4.4 %collective-permute-done.20 = f32[2,256,512]{2,1,0:T(8,128)S(1)} collective-permute-done((f32[2,256,512]{2,1,0:T(8,128)S(1)}, f32[2,256,512]{2,1,0:T(8,128)S(1)}, u32[]{:S(2)}, u32[]{:S(2)}) %collective-permute-start.20) | collective-permute-done | bytes 1048608 | tf_op jit(solution)/shard_map/ppermute | solution.py:403
  272.1 22.5 %collective-permute-done.10 = f32[2,256,512]{2,1,0:T(8,128)S(1)} collective-permute-done((f32[2,256,512]{2,1,0:T(8,128)S(1)}, f32[2,256,512]{2,1,0:T(8,128)S(1)}, u32[]{:S(2)}, u32[]{:S(2)}) %collective-permute-start.10) | collective-permute-done | bytes 1048608 | tf_op jit(solution)/shard_map/ppermute | solution.py:403
  295.2 5.5 %collective-permute-start.21 = (f32[512,128]{1,0:T(8,128)S(1)}, f32[512,128]{1,0:T(8,128)S(1)}, u32[]{:S(2)}, u32[]{:S(2)}) collective-permute-start(f32[512,128]{1,0:T(8,128)S(1)} %get-tuple-element.51), channel_id=1, source_target_pairs={{0,1},{1,2},{2,3},{3,4},{4,5},{5,6},{6,7},{8,9},{9,10},{10,11},{11... | collective-permute-start | bytes 786440 | tf_op jit(solution)/shard_map/ppermute | solution.py:403
  303.6 2.3 taps.1.t_ref
  305.9 2.5 collective-permute-done.22.right
  309.0 3.9 %columns.1.f_ref = f32[512,512]{1,0:T(8,128)} custom-call(f32[512,512]{1,0:T(8,128)} %bitcast.111, f32[512,128]{1,0:T(8,128)} %copy-done.13, f32[512,128]{1,0:T(8,128)} %copy-done.14, bf16[2,2,512,512]{3,2,1,0:T(8,128)(2,1)} %taps.1.t_ref), custom_call_target="tpu_custom_call" | custom-call | tf_op jit(solution)/shard_map/columns/pallas_call | solution.py:368
  313.8 4.8 %collective-permute-start.24 = (f32[24,512]{1,0:T(8,128)S(1)}, f32[24,512]{1,0:T(8,128)S(1)}, u32[]{:S(2)}, u32[]{:S(2)}) collective-permute-start(f32[24,512]{1,0:T(8,128)S(1)} %get-tuple-element.48), channel_id=1, source_target_pairs={{0,120},{8,0},{16,8},{24,16},{32,24},{40,32},{48,40},{56,48},{64,5... | collective-permute-start | bytes 147464 | tf_op jit(solution)/shard_map/ppermute | solution.py:403
  321.3 3.7 %rows.1 = f32[512,512]{1,0:T(8,128)} custom-call(f32[512,512]{1,0:T(8,128)} %columns.1.f_ref, f32[24,512]{1,0:T(8,128)} %copy-done.15, f32[24,512]{1,0:T(8,128)} %copy-done.16, bf16[2,2,512,512]{3,2,1,0:T(8,128)(2,1)} %taps.1.t_ref), custom_call_target="tpu_custom_call" | custom-call | tf_op jit(solution)/shard_map/rows/pallas_call | solution.py:384
  (109 shorter events, 39.2 us)
Async XLA Ops:
  14.2 107.1 %collective-permute-start.11 = (f32[16,256,256]{2,1,0:T(8,128)}, f32[16,256,256]{2,1,0:T(8,128)}, u32[]{:S(2)}, u32[]{:S(2)}) collective-permute-start(f32[16,256,256]{2,1,0:T(8,128)} %get-tuple-element.39), channel_id=1, source_target_pairs={{0,1},{1,0},{2,3},{3,2},{4,5},{5,4},{6,7},{7,6},{8,9},{9,8},{10,11... | collective-permute-start | bytes 12582920 | tf_op jit(solution)/shard_map/ppermute | solution.py:407
  113.7 17.4 %collective-permute-start.1 = (f32[16,256,256]{2,1,0:T(8,128)}, f32[16,256,256]{2,1,0:T(8,128)}, u32[]{:S(2)}, u32[]{:S(2)}) collective-permute-start(f32[16,256,256]{2,1,0:T(8,128)} %get-tuple-element.29), channel_id=1, source_target_pairs={{0,1},{1,0},{2,3},{3,2},{4,5},{5,4},{6,7},{7,6},{8,9},{9,8},{10,11... | collective-permute-start | bytes 12582920 | tf_op jit(solution)/shard_map/ppermute | solution.py:407
  113.8 7.5 %collective-permute-start = (s32[48]{0:T(128)S(1)}, s32[48]{0:T(128)S(1)}, u32[]{:S(2)}, u32[]{:S(2)}) collective-permute-start(s32[48]{0:T(128)S(1)} %copy-done.23), channel_id=1, source_target_pairs={{0,1},{1,0},{2,3},{3,2},{4,5},{5,4},{6,7},{7,6},{8,9},{9,8},{10,11... | collective-permute-start | bytes 584 | tf_op jit(solution)/shard_map/ppermute | solution.py:407
  128.4 26.0 %collective-permute-start.16 = (f32[2,256,512]{2,1,0:T(8,128)}, f32[2,256,512]{2,1,0:T(8,128)S(1)}, u32[]{:S(2)}, u32[]{:S(2)}) collective-permute-start(f32[2,256,512]{2,1,0:T(8,128)} %get-tuple-element.46), channel_id=1, source_target_pairs={{0,2},{1,3},{2,4},{3,5},{4,6},{5,7},{6,0},{7,1},{8,10},{9,11},{10,... | collective-permute-start | bytes 3145736 | tf_op jit(solution)/shard_map/ppermute | solution.py:403
  129.8 26.3 %collective-permute-start.18 = (f32[2,256,512]{2,1,0:T(8,128)}, f32[2,256,512]{2,1,0:T(8,128)}, u32[]{:S(2)}, u32[]{:S(2)}) collective-permute-start(f32[2,256,512]{2,1,0:T(8,128)} %get-tuple-element.47), channel_id=1, source_target_pairs={{0,6},{1,7},{2,0},{3,1},{4,2},{5,3},{6,4},{7,5},{8,14},{9,15},{10,... | collective-permute-start | bytes 3145736 | tf_op jit(solution)/shard_map/ppermute | solution.py:403
  137.6 39.3 %collective-permute-start.6 = (f32[2,256,512]{2,1,0:T(8,128)}, f32[2,256,512]{2,1,0:T(8,128)}, u32[]{:S(2)}, u32[]{:S(2)}) collective-permute-start(f32[2,256,512]{2,1,0:T(8,128)} %get-tuple-element.36), channel_id=1, source_target_pairs={{0,2},{1,3},{2,4},{3,5},{4,6},{5,7},{6,0},{7,1},{8,10},{9,11},{10,... | collective-permute-start | bytes 3145736 | tf_op jit(solution)/shard_map/ppermute | solution.py:403
  137.9 39.8 %collective-permute-start.8 = (f32[2,256,512]{2,1,0:T(8,128)}, f32[2,256,512]{2,1,0:T(8,128)}, u32[]{:S(2)}, u32[]{:S(2)}) collective-permute-start(f32[2,256,512]{2,1,0:T(8,128)} %get-tuple-element.37), channel_id=1, source_target_pairs={{0,6},{1,7},{2,0},{3,1},{4,2},{5,3},{6,4},{7,5},{8,14},{9,15},{10,... | collective-permute-start | bytes 3145736 | tf_op jit(solution)/shard_map/ppermute | solution.py:403
  146.7 52.6 %collective-permute-start.12 = (f32[2,256,512]{2,1,0:T(8,128)}, f32[2,256,512]{2,1,0:T(8,128)S(1)}, u32[]{:S(2)}, u32[]{:S(2)}) collective-permute-start(f32[2,256,512]{2,1,0:T(8,128)} %get-tuple-element.42), channel_id=1, source_target_pairs={{0,2},{1,3},{2,4},{3,5},{4,6},{5,7},{6,0},{7,1},{8,10},{9,11},{10,... | collective-permute-start | bytes 3145736 | tf_op jit(solution)/shard_map/ppermute | solution.py:403
  154.4 46.7 %collective-permute-start.14 = (f32[2,256,512]{2,1,0:T(8,128)}, f32[2,256,512]{2,1,0:T(8,128)}, u32[]{:S(2)}, u32[]{:S(2)}) collective-permute-start(f32[2,256,512]{2,1,0:T(8,128)} %get-tuple-element.43), channel_id=1, source_target_pairs={{0,6},{1,7},{2,0},{3,1},{4,2},{5,3},{6,4},{7,5},{8,14},{9,15},{10,... | collective-permute-start | bytes 3145736 | tf_op jit(solution)/shard_map/ppermute | solution.py:403
  158.3 52.3 %collective-permute-start.17 = (f32[256,512]{1,0:T(8,128)}, f32[256,512]{1,0:T(8,128)}, u32[]{:S(2)}, u32[]{:S(2)}) collective-permute-start(f32[256,512]{1,0:T(8,128)} %get-tuple-element.58), channel_id=1, source_target_pairs={{0,2},{1,3},{2,4},{3,5},{4,6},{5,7},{6,0},{7,1},{8,10},{9,11},{10,... | collective-permute-start | bytes 1572872 | tf_op jit(solution)/shard_map/ppermute | solution.py:403
  176.9 71.9 %collective-permute-start.2 = (f32[2,256,512]{2,1,0:T(8,128)}, f32[2,256,512]{2,1,0:T(8,128)S(1)}, u32[]{:S(2)}, u32[]{:S(2)}) collective-permute-start(f32[2,256,512]{2,1,0:T(8,128)} %get-tuple-element.32), channel_id=1, source_target_pairs={{0,2},{1,3},{2,4},{3,5},{4,6},{5,7},{6,0},{7,1},{8,10},{9,11},{10,... | collective-permute-start | bytes 3145736 | tf_op jit(solution)/shard_map/ppermute | solution.py:403
  177.6 36.0 %collective-permute-start.19 = (f32[256,512]{1,0:T(8,128)}, f32[256,512]{1,0:T(8,128)S(1)}, u32[]{:S(2)}, u32[]{:S(2)}) collective-permute-start(f32[256,512]{1,0:T(8,128)} %get-tuple-element.59), channel_id=1, source_target_pairs={{0,6},{1,7},{2,0},{3,1},{4,2},{5,3},{6,4},{7,5},{8,14},{9,15},{10,... | collective-permute-start | bytes 1572872 | tf_op jit(solution)/shard_map/ppermute | solution.py:403
  199.3 51.0 %collective-permute-start.4 = (f32[2,256,512]{2,1,0:T(8,128)}, f32[2,256,512]{2,1,0:T(8,128)S(1)}, u32[]{:S(2)}, u32[]{:S(2)}) collective-permute-start(f32[2,256,512]{2,1,0:T(8,128)} %get-tuple-element.33), channel_id=1, source_target_pairs={{0,6},{1,7},{2,0},{3,1},{4,2},{5,3},{6,4},{7,5},{8,14},{9,15},{10,... | collective-permute-start | bytes 3145736 | tf_op jit(solution)/shard_map/ppermute | solution.py:403
  201.0 43.2 %collective-permute-start.7 = (f32[256,512]{1,0:T(8,128)S(1)}, f32[256,512]{1,0:T(8,128)S(1)}, u32[]{:S(2)}, u32[]{:S(2)}) collective-permute-start(f32[256,512]{1,0:T(8,128)S(1)} %get-tuple-element.66), channel_id=1, source_target_pairs={{0,2},{1,3},{2,4},{3,5},{4,6},{5,7},{6,0},{7,1},{8,10},{9,11},{10,... | collective-permute-start | bytes 1572872 | tf_op jit(solution)/shard_map/ppermute | solution.py:403
  210.6 35.2 %collective-permute-start.9 = (f32[256,512]{1,0:T(8,128)S(1)}, f32[256,512]{1,0:T(8,128)S(1)}, u32[]{:S(2)}, u32[]{:S(2)}) collective-permute-start(f32[256,512]{1,0:T(8,128)S(1)} %get-tuple-element.67), channel_id=1, source_target_pairs={{0,6},{1,7},{2,0},{3,1},{4,2},{5,3},{6,4},{7,5},{8,14},{9,15},{10,... | collective-permute-start | bytes 1572872 | tf_op jit(solution)/shard_map/ppermute | solution.py:403
  213.6 41.8 %collective-permute-start.13 = (f32[256,512]{1,0:T(8,128)S(1)}, f32[256,512]{1,0:T(8,128)S(1)}, u32[]{:S(2)}, u32[]{:S(2)}) collective-permute-start(f32[256,512]{1,0:T(8,128)S(1)} %get-tuple-element.54), channel_id=1, source_target_pairs={{0,2},{1,3},{2,4},{3,5},{4,6},{5,7},{6,0},{7,1},{8,10},{9,11},{10,... | collective-permute-start | bytes 1572872 | tf_op jit(solution)/shard_map/ppermute | solution.py:403
  244.2 12.9 %collective-permute-start.15 = (f32[256,512]{1,0:T(8,128)S(1)}, f32[256,512]{1,0:T(8,128)S(1)}, u32[]{:S(2)}, u32[]{:S(2)}) collective-permute-start(f32[256,512]{1,0:T(8,128)S(1)} %get-tuple-element.55), channel_id=1, source_target_pairs={{0,6},{1,7},{2,0},{3,1},{4,2},{5,3},{6,4},{7,5},{8,14},{9,15},{10,... | collective-permute-start | bytes 1572872 | tf_op jit(solution)/shard_map/ppermute | solution.py:403
  245.9 26.3 %collective-permute-start.20 = (f32[2,256,512]{2,1,0:T(8,128)S(1)}, f32[2,256,512]{2,1,0:T(8,128)S(1)}, u32[]{:S(2)}, u32[]{:S(2)}) collective-permute-start(f32[2,256,512]{2,1,0:T(8,128)S(1)} %pad_maximum_fusion.1), channel_id=1, source_target_pairs={{0,8},{8,16},{16,24},{24,32},{32,40},{40,48},{48,56},{56,64},{64,7... | collective-permute-start | bytes 3145736 | tf_op jit(solution)/shard_map/ppermute | solution.py:403
  248.8 45.8 %collective-permute-start.10 = (f32[2,256,512]{2,1,0:T(8,128)S(1)}, f32[2,256,512]{2,1,0:T(8,128)S(1)}, u32[]{:S(2)}, u32[]{:S(2)}) collective-permute-start(f32[2,256,512]{2,1,0:T(8,128)S(1)} %pad_maximum_fusion), channel_id=1, source_target_pairs={{0,8},{8,16},{16,24},{24,32},{32,40},{40,48},{48,56},{56,64},{64,7... | collective-permute-start | bytes 3145736 | tf_op jit(solution)/shard_map/ppermute | solution.py:403
  250.5 16.2 %collective-permute-start.3 = (f32[256,512]{1,0:T(8,128)S(1)}, f32[256,512]{1,0:T(8,128)S(1)}, u32[]{:S(2)}, u32[]{:S(2)}) collective-permute-start(f32[256,512]{1,0:T(8,128)S(1)} %get-tuple-element.62), channel_id=1, source_target_pairs={{0,2},{1,3},{2,4},{3,5},{4,6},{5,7},{6,0},{7,1},{8,10},{9,11},{10,... | collective-permute-start | bytes 1572872 | tf_op jit(solution)/shard_map/ppermute | solution.py:403
  255.5 11.8 %collective-permute-start.5 = (f32[256,512]{1,0:T(8,128)S(1)}, f32[256,512]{1,0:T(8,128)S(1)}, u32[]{:S(2)}, u32[]{:S(2)}) collective-permute-start(f32[256,512]{1,0:T(8,128)S(1)} %get-tuple-element.63), channel_id=1, source_target_pairs={{0,6},{1,7},{2,0},{3,1},{4,2},{5,3},{6,4},{7,5},{8,14},{9,15},{10,... | collective-permute-start | bytes 1572872 | tf_op jit(solution)/shard_map/ppermute | solution.py:403
  295.2 10.7 %collective-permute-start.21 = (f32[512,128]{1,0:T(8,128)S(1)}, f32[512,128]{1,0:T(8,128)S(1)}, u32[]{:S(2)}, u32[]{:S(2)}) collective-permute-start(f32[512,128]{1,0:T(8,128)S(1)} %get-tuple-element.51), channel_id=1, source_target_pairs={{0,1},{1,2},{2,3},{3,4},{4,5},{5,6},{6,7},{8,9},{9,10},{10,11},{11... | collective-permute-start | bytes 786440 | tf_op jit(solution)/shard_map/ppermute | solution.py:403
  300.6 7.7 %collective-permute-start.22 = (f32[512,128]{1,0:T(8,128)S(1)}, f32[512,128]{1,0:T(8,128)S(1)}, u32[]{:S(2)}, u32[]{:S(2)}) collective-permute-start(f32[512,128]{1,0:T(8,128)S(1)} %get-tuple-element.50), channel_id=1, source_target_pairs={{1,0},{2,1},{3,2},{4,3},{5,4},{6,5},{7,6},{9,8},{10,9},{11,10},{12... | collective-permute-start | bytes 786440 | tf_op jit(solution)/shard_map/ppermute | solution.py:403
  313.8 6.3 %collective-permute-start.23 = (f32[24,512]{1,0:T(8,128)S(1)}, f32[24,512]{1,0:T(8,128)S(1)}, u32[]{:S(2)}, u32[]{:S(2)}) collective-permute-start(f32[24,512]{1,0:T(8,128)S(1)} %get-tuple-element.49), channel_id=1, source_target_pairs={{0,8},{8,16},{16,24},{24,32},{32,40},{40,48},{48,56},{56,64},{64,7... | collective-permute-start | bytes 147464 | tf_op jit(solution)/shard_map/ppermute | solution.py:403
  (25 other events, 566.8 us)
